TPU v7x, 512 devices: a whole 4x4x16 slice. The times are simulated.
512 devices in a mesh: section: 8 (over y_hi, x), head: 4 (over y_lo, core), tok: 16 (over z).
Axes of the slice: x: 4, y: 4 (y_hi: 2, y_lo: 2; y = y_hi * 2 + y_lo), z: 16, core: 2. Of those that a mesh axis runs over, the one named last changes fastest.
Arguments:
- held_cotangents: bfloat16 [8, 2, 2048, 2560], P('section', None, 'tok', 'head'), may hold values from -6 to 6
- entering_adjoint: bfloat16 [2048, 2560], P('tok', 'head'), may hold values from -6 to 6
- saved_queries: bfloat16 [8, 2048, 2560], P('section', 'tok', 'head'), may hold values from -1024 to 1024
- saved_keys: bfloat16 [8, 2048, 2560], P('section', 'tok', 'head'), may hold values from -20 to 20
- value_weight: bfloat16 [8, 2560, 2560], P('section', None, 'head'), may hold values from -0.125 to 0.125
- out_weight: bfloat16 [8, 2560, 2560], P('section', 'tok', 'head'), may hold values from -0.125 to 0.125
- block_gate: float32 [8, 2560], P('section'), may hold values from -3 to 3
- time_gate: float32 [32, 2560], replicated, may hold values from -3 to 3
- timestep: int32 [1], replicated, may hold values from 0 to 31
Outputs:
- passed: bfloat16 [8, 2, 2048, 2560], P('section', None, 'tok', 'head')
All inputs are finite; a program needn't handle non-finite values.
Results may differ from a plain program's by a relative error of at most 0.0085.
Values may be sent and summed in bfloat16 or wider, within the bound.
A program may use at most 64 MiB of HBM per device.

v0:
```python
import jax
import jax.numpy as jnp
from jax import lax
from jax.sharding import PartitionSpec as P

HD = 128
GUIDE = 3.0


def shifted(value, axis, steps):
    count = lax.axis_size(axis)
    leading, last = (max(0, -steps), min(count, count - steps))
    return lax.ppermute(value, axis, [(source, source + steps) for source in range(leading, last)])


def shards(
    held_cotangents,
    entering_adjoint,
    saved_queries,
    saved_keys,
    value_weight,
    out_weight,
    block_gate,
    time_gate,
    timestep,
):
    steps_index = jnp.arange(time_gate.shape[0])
    time_row = jnp.sum(
        jnp.where((steps_index == timestep[0])[:, None], time_gate, jnp.zeros_like(time_gate)),
        axis=0,
    )
    gate_row = block_gate[0] + time_row
    whole_cot = lax.all_gather(held_cotangents[0], "head", axis=2, tiled=True)
    scaled = (whole_cot.astype(jnp.float32) * gate_row).astype(jnp.bfloat16)
    out_full = lax.all_gather(out_weight[0], "tok", axis=0, tiled=True)
    attn_grad = jnp.einsum(
        "btd,dk->btk", scaled, out_full, preferred_element_type=jnp.float32
    ).astype(jnp.bfloat16)
    rows_here = saved_queries.shape[1]
    groups_here = saved_queries.shape[2] // HD
    score_scale = HD ** (-0.5)
    normal_grad = attn_grad[0]
    key_all = lax.all_gather(saved_keys[0], "tok", axis=0, tiled=True)
    key_heads = key_all.reshape(key_all.shape[0], groups_here, HD)
    query_heads = saved_queries[0].reshape(rows_here, groups_here, HD)
    scores = (
        jnp.einsum("ihe,jhe->hij", query_heads, key_heads, preferred_element_type=jnp.float32)
        * score_scale
    )
    row_top = jnp.max(scores, axis=2, keepdims=True)
    log_total = row_top + jnp.log(jnp.sum(jnp.exp(scores - row_top), axis=2, keepdims=True))
    weights = jnp.exp(scores - log_total).astype(jnp.bfloat16)
    grad_heads = normal_grad.reshape(rows_here, groups_here, HD)
    terms = jnp.einsum("hij,ihe->jhe", weights, grad_heads, preferred_element_type=jnp.float32)
    value_grad = lax.psum_scatter(
        terms.reshape(lax.axis_size("tok") * rows_here, groups_here * HD).astype(jnp.bfloat16),
        "tok",
        scatter_dimension=0,
        tiled=True,
    )
    stacked = jnp.stack([value_grad, attn_grad[1]])
    partial_back = jnp.einsum(
        "btk,dk->btd", stacked, value_weight[0], preferred_element_type=jnp.float32
    )
    back_sum = lax.psum_scatter(
        partial_back.astype(jnp.bfloat16), "head", scatter_dimension=2, tiled=True
    ).astype(jnp.float32)
    block_cot = (held_cotangents[0].astype(jnp.float32) + back_sum).astype(jnp.bfloat16)
    passed_on = shifted(block_cot, "section", -1)
    entering_full = entering_adjoint.astype(jnp.float32)
    fresh_rows = jnp.stack([(1.0 + GUIDE) * entering_full, -GUIDE * entering_full]).astype(
        jnp.bfloat16
    )
    is_last = lax.axis_index("section") == lax.axis_size("section") - 1
    return jnp.where(is_last, fresh_rows, passed_on)[None]


def solution(mesh):
    return jax.shard_map(
        shards,
        mesh=mesh,
        in_specs=(
            P("section", None, "tok", "head"),
            P("tok", "head"),
            P("section", "tok", "head"),
            P("section", "tok", "head"),
            P("section", None, "head"),
            P("section", "tok", "head"),
            P("section", None),
            P(),
            P(),
        ),
        out_specs=P("section", None, "tok", "head"),
        check_vma=False,
    )
```

profile of v0, /device:TPU:6, one launch (start us, length us, event | category | flops | bytes accessed | tf_op | source)
XLA Modules:
  0.0 357.0 jit_solution(16926532515218221262)
XLA Ops:
  6.5 0.0 copy-start
  6.5 0.0 all-gather.11.cloned.1.call-start
  6.5 1.9 copy.21
  8.4 0.0 all-gather.11.cloned.1.call-update
  8.4 0.0 all-gather.7.cloned.1.call-start
  8.5 0.7 all-gather.7.cloned.1.call-update
  9.2 0.0 all-gather.9.cloned.1.call-start
  9.2 0.7 all-gather.9.cloned.1.call-update
  9.9 0.0 reduce-scatter.5.cloned.1.call-start
  10.6 1.1 copy.20
  11.7 0.7 reduce
  12.4 1.1 select_reduce_fusion
  13.5 83.0 %all-gather.11.cloned.1.call-done = bf16[1,2048,640]{1,2,0:T(8,128)(2,1)} async-done(((bf16[1,128,640]{1,2,0:T(8,128)(2,1)}), bf16[1,2048,640]{1,2,0:T(8,128)(2,1)}) %all-gather.11.cloned.1.call-update) | async-done | bytes 2621456 | tf_op jit(solution)/shard_map/all_gather | solution.py:43
  96.6 2.7 multiply_reduce_fusion
  99.3 0.0 copy-start.1
  99.3 2.3 copy-done.1
  101.6 1.0 exponential_reduce_fusion
  102.6 21.9 %all-gather.7.cloned.1.call-done = bf16[1,2,128,2560]{3,2,1,0:T(8,128)(2,1)} async-done(((bf16[1,2,128,640]{3,2,1,0:T(8,128)(2,1)}), bf16[1,2,128,2560]{3,2,1,0:T(8,128)(2,1)}) %all-gather.7.cloned.1.call-update) | async-done | bytes 1310736 | tf_op jit(solution)/shard_map/all_gather | solution.py:33
  124.5 79.6 %all-gather.9.cloned.1.call-done = bf16[1,2560,640]{2,1,0:T(8,128)(2,1)} async-done(((bf16[1,160,640]{2,1,0:T(8,128)(2,1)}), bf16[1,2560,640]{2,1,0:T(8,128)(2,1)}) %all-gather.9.cloned.1.call-update) | async-done | bytes 3276816 | tf_op jit(solution)/shard_map/all_gather | solution.py:35
  204.2 3.5 fusion.9
  207.7 0.7 fusion.25
  208.4 0.8 copy.19
  209.2 5.3 %convolution_convert_fusion.1 = bf16[5,128,2048]{2,1,0:T(8,128)(2,1)} fusion(bf16[128,5,128]{0,2,1:T(8,128)(2,1)} %bitcast.51, f32[5,128,2048]{2,1,0:T(8,128)} %copy-done.1, f32[5,128]{1,0:T(8,128)S(1)} %log_add_fusion), kind=kOutput, calls=%fused_computation.7 | convolution fusion | flops 340787200 | bytes 8030720 | tf_op jit(solution)/shard_map/hij,ihe->jhe/dot_general | solution.py:54
  214.5 0.0 copy-start.2
  214.5 4.4 %copy.24 = bf16[2048,640]{1,0:T(8,128)(2,1)} copy(bf16[2048,640]{0,1:T(8,128)(2,1)} %bitcast.45) | data formatting | bytes 5242880 | tf_op jit(solution)/shard_map/convert_element_type | solution.py:56
  218.9 0.0 reduce-scatter.5.cloned.1.call-update
  218.9 0.0 reduce-scatter.7.cloned.1.call-start
  219.0 71.2 %reduce-scatter.5.cloned.1.call-done = bf16[128,640]{1,0:T(8,128)(2,1)} async-done(((bf16[2048,640]{1,0:T(8,128)(2,1)}), bf16[128,640]{1,0:T(8,128)(2,1)}) %reduce-scatter.5.cloned.1.call-update) | async-done | bytes 163856 | tf_op jit(solution)/shard_map/reduce_scatter | solution.py:55
  290.2 0.0 copy-done
  290.2 0.0 copy-done.2
  290.2 3.2 convolution_convert_fusion
  293.4 4.3 %copy.27 = bf16[2,128,2560]{1,0,2:T(2,128)(2,1)} copy(bf16[2,128,2560]{2,1,0:T(8,128)(2,1)} %convolution_convert_fusion) | data formatting | bytes 2621440
  297.7 0.0 copy-start.3
  297.7 2.6 copy.31
  300.3 0.0 reduce-scatter.7.cloned.1.call-update
  300.3 27.3 %reduce-scatter.7.cloned.1.call-done = bf16[640,256]{1,0:T(8,128)(2,1)} async-done(((bf16[2560,256]{1,0:T(8,128)(2,1)}), bf16[640,256]{1,0:T(8,128)(2,1)}) %reduce-scatter.7.cloned.1.call-update) | async-done | bytes 327696
  327.6 1.8 reshape.35
  329.4 1.9 copy.28
  331.3 1.9 fusion.14
  333.2 2.7 collective-permute-start
  336.0 0.0 copy-done.3
  336.0 12.7 %collective-permute-done = bf16[2,128,640]{2,1,0:T(8,128)(2,1)} collective-permute-done((bf16[2,128,640]{2,1,0:T(8,128)(2,1)}, bf16[2,128,640]{2,1,0:T(8,128)(2,1)}, u32[]{:S(2)}, u32[]{:S(2)}) %collective-permute-start) | collective-permute-done | bytes 327712 | tf_op jit(solution)/shard_map/ppermute | solution.py:13
  348.8 1.7 fusion.17
  (4 shorter events, 0.1 us)
Async XLA Ops:
  6.5 283.7 %copy-start = (bf16[1,2560,640]{2,1,0:T(8,128)(2,1)S(1)}, bf16[1,2560,640]{2,1,0:T(8,128)(2,1)}, u32[]{:S(2)}) copy-start(bf16[1,2560,640]{2,1,0:T(8,128)(2,1)} %param.13) | copy-start | bytes 9830404
  6.5 90.0 %all-gather.11.cloned.1.call-start = ((), (), s32[]{:S(2)}) async-start(), calls=%async_computation.5 | async-start | bytes 2785280 | tf_op jit(solution)/shard_map/all_gather | solution.py:43
  8.4 116.1 %all-gather.7.cloned.1.call-start = ((), (), s32[]{:S(2)}) async-start(), calls=%async_computation.3 | async-start | bytes 1638400 | tf_op jit(solution)/shard_map/all_gather | solution.py:33
  9.2 195.0 %all-gather.9.cloned.1.call-start = ((), (), s32[]{:S(2)}) async-start(), calls=%async_computation.4 | async-start | bytes 3481600 | tf_op jit(solution)/shard_map/all_gather | solution.py:35
  9.9 280.3 %reduce-scatter.5.cloned.1.call-start = ((), (), s32[]{:S(2)}) async-start(), calls=%async_computation.2 | async-start | bytes 2785280 | tf_op jit(solution)/shard_map/reduce_scatter | solution.py:55
  99.3 2.3 copy-start.1
  214.5 75.7 %copy-start.2 = (bf16[1,128,640]{2,1,0:T(8,128)(2,1)S(1)}, bf16[1,128,640]{2,1,0:T(8,128)(2,1)}, u32[]{:S(2)}) copy-start(bf16[1,128,640]{2,1,0:T(8,128)(2,1)} %get-tuple-element.6) | copy-start | bytes 491524
  218.9 108.7 %reduce-scatter.7.cloned.1.call-start = ((), (), s32[]{:S(2)}) async-start(), calls=%async_computation.6 | async-start | bytes 1638400
  297.7 38.3 %copy-start.3 = (bf16[128,640]{1,0:T(8,128)(2,1)S(1)}, bf16[128,640]{1,0:T(8,128)(2,1)}, u32[]{:S(2)}) copy-start(bf16[128,640]{1,0:T(8,128)(2,1)} %param.10) | copy-start | bytes 491524
  333.2 15.6 %collective-permute-start = (bf16[2,128,640]{2,1,0:T(8,128)(2,1)}, bf16[2,128,640]{2,1,0:T(8,128)(2,1)}, u32[]{:S(2)}, u32[]{:S(2)}) collective-permute-start(bf16[2,128,640]{2,1,0:T(8,128)(2,1)} %fusion.14), channel_id=1, source_target_pairs={{64,0},{128,64},{192,128},{256,192},{320,256},{384,320},{448,384},... | collective-permute-start | bytes 983048 | tf_op jit(solution)/shard_map/ppermute | solution.py:13
Sparse Core Ops, SparseCore 0:
  9.4 87.1 all-gather.10
  98.7 25.7 all-gather.6
  126.6 77.5 all-gather.8
  219.1 71.0 reduce-scatter.4
  300.4 27.1 reduce-scatter.6
where the time goes:
time: 358 us; the launch traced here: 357 us
  waiting for transfers between devices  297 us (83%)
  local copies, waits for them, and re-layouts  21.7 us (6%)
  matrix products  14.7 us (4%)
  between operations  13.9 us (4%)
  other arithmetic  6.49 us (2%)
    all_gather x1, waiting for transfers between devices, shards(): key_all = lax.all_gather(saved_keys[0], 'tok', axis=0, tiled=True)  83 us
    all_gather x1, waiting for transfers between devices, shards(): out_full = lax.all_gather(out_weight[0], 'tok', axis=0, tiled=True)  79.6 us
    reduce_scatter x1, waiting for transfers between devices, shards(): lax.psum_scatter(terms.reshape(lax.axis_size('tok') * rows_here, groups_h...  71.2 us
    unnamed x6, waiting for transfers between devices  28.7 us
    all_gather x1, waiting for transfers between devices, shards(): whole_cot = lax.all_gather(held_cotangents[0], 'head', axis=2, tiled=True)  21.9 us
    unnamed x14, local copies, waits for them, and re-layouts  15.8 us
    ppermute x1, waiting for transfers between devices, shifted(): lax.ppermute(value, axis, [(source, source + steps) for source in range(l...  12.7 us
  transfers between devices with their start and end apart: 6, of which 6 were waited for; matrix products, arithmetic and copies ran while one was open for 2% of the time, Pallas kernels for 0%

commit v1 on v0

--- a/solution.py
+++ b/solution.py
@@ -40,7 +40,12 @@
     groups_here = saved_queries.shape[2] // HD
     score_scale = HD ** (-0.5)
     normal_grad = attn_grad[0]
-    key_all = lax.all_gather(saved_keys[0], "tok", axis=0, tiled=True)
+    ring = [saved_keys[0]]
+    for hop in range(15):
+        ring.append(lax.ppermute(ring[-1], "tok", [(dev, (dev + 1) % 16) for dev in range(16)]))
+    key_all = jnp.roll(
+        jnp.concatenate(ring[::-1], axis=0), (lax.axis_index("tok") + 1) * ring[0].shape[0], axis=0
+    )
     key_heads = key_all.reshape(key_all.shape[0], groups_here, HD)
     query_heads = saved_queries[0].reshape(rows_here, groups_here, HD)
     scores = (

time: 358 us -> 341 us (0.953)
  waiting for transfers between devices: 297 us -> 223 us
  starting transfers between devices: 2.91 us -> 33.4 us
  local copies, waits for them, and re-layouts: 21.7 us -> 48.4 us
    ppermute x0 -> x15, waiting for transfers between devices: none -> 109 us  [shards(): lax.ppermute(ring[-1], 'tok', [(dev, (dev + 1) % 16) for dev in range(16)])]
    all_gather x1 -> x0, waiting for transfers between devices: 83 us -> none  [shards(): key_all = lax.all_gather(saved_keys[0], 'tok', axis=0, tiled=True)]
    all_gather x1, waiting for transfers between devices: 79.6 us -> 2.98 us  [shards(): out_full = lax.all_gather(out_weight[0], 'tok', axis=0, tiled=True)]
    ppermute x0 -> x15, starting transfers between devices: none -> 30.5 us  [shards(): lax.ppermute(ring[-1], 'tok', [(dev, (dev + 1) % 16) for dev in range(16)])]
    unnamed x14 -> x89, local copies, waits for them, and re-layouts: 15.8 us -> 42.2 us
    all_gather x1, waiting for transfers between devices: 21.9 us -> 0.02 us  [shards(): whole_cot = lax.all_gather(held_cotangents[0], 'head', axis=2, tiled=True)]
    unnamed x6 -> x5, waiting for transfers between devices: 28.7 us -> 28.2 us
  transfers between devices with their start and end apart: 6 -> 20, of which waited for: 6 -> 19; matrix products, arithmetic and copies ran while one was open for 2% -> 8% of each run, Pallas kernels for 0% -> 0%
where the time goes in v1:
time: 341 us; the launch traced here: 340 us
  waiting for transfers between devices  223 us (65%)
  local copies, waits for them, and re-layouts  48.4 us (14%)
  starting transfers between devices  33.4 us (10%)
  between operations  14.5 us (4%)
  matrix products  13 us (4%)
  other arithmetic  7.43 us (2%)
    ppermute x15, waiting for transfers between devices, shards(): lax.ppermute(ring[-1], 'tok', [(dev, (dev + 1) % 16) for dev in range(16)])  109 us
    reduce_scatter x1, waiting for transfers between devices, shards(): lax.psum_scatter(terms.reshape(lax.axis_size('tok') * rows_here, groups_h...  71 us
    unnamed x89, local copies, waits for them, and re-layouts  42.2 us
    ppermute x15, starting transfers between devices, shards(): lax.ppermute(ring[-1], 'tok', [(dev, (dev + 1) % 16) for dev in range(16)])  30.5 us
    unnamed x5, waiting for transfers between devices  28.2 us
    ppermute x1, waiting for transfers between devices, shifted(): lax.ppermute(value, axis, [(source, source + steps) for source in range(l...  11.8 us
  transfers between devices with their start and end apart: 20, of which 19 were waited for; matrix products, arithmetic and copies ran while one was open for 8% of the time, Pallas kernels for 0%

profile of v1, /device:TPU:6, one launch (start us, length us, event | category | flops | bytes accessed | tf_op | source)
XLA Modules:
  0.0 339.8 jit_solution(2083810573175047715)
XLA Ops:
  7.3 1.3 copy.22
  8.6 3.8 %collective-permute-start = (bf16[128,640]{0,1:T(8,128)(2,1)S(1)}, bf16[128,640]{0,1:T(8,128)(2,1)S(1)}, u32[]{:S(2)}, u32[]{:S(2)}) collective-permute-start(bf16[128,640]{0,1:T(8,128)(2,1)S(1)} %bitcast.65), channel_id=1, source_target_pairs={{0,1},{1,2},{2,3},{3,4},{4,5},{5,6},{6,7},{7,8},{8,9},{9,10},{10,1... | collective-permute-start | bytes 491528 | tf_op jit(solution)/shard_map/ppermute | solution.py:45
  12.4 11.8 %collective-permute-done = bf16[128,640]{0,1:T(8,128)(2,1)S(1)} collective-permute-done((bf16[128,640]{0,1:T(8,128)(2,1)S(1)}, bf16[128,640]{0,1:T(8,128)(2,1)S(1)}, u32[]{:S(2)}, u32[]{:S(2)}) %collective-permute-start) | collective-permute-done | bytes 163872 | tf_op jit(solution)/shard_map/ppermute | solution.py:45
  24.8 1.9 collective-permute-start.1
  26.8 6.6 %collective-permute-done.1 = bf16[128,640]{0,1:T(8,128)(2,1)S(1)} collective-permute-done((bf16[128,640]{0,1:T(8,128)(2,1)S(1)}, bf16[128,640]{0,1:T(8,128)(2,1)S(1)}, u32[]{:S(2)}, u32[]{:S(2)}) %collective-permute-start.1) | collective-permute-done | bytes 163872 | tf_op jit(solution)/shard_map/ppermute | solution.py:45
  34.0 1.9 collective-permute-start.2
  35.9 6.5 %collective-permute-done.2 = bf16[128,640]{0,1:T(8,128)(2,1)S(1)} collective-permute-done((bf16[128,640]{0,1:T(8,128)(2,1)S(1)}, bf16[128,640]{0,1:T(8,128)(2,1)S(1)}, u32[]{:S(2)}, u32[]{:S(2)}) %collective-permute-start.2) | collective-permute-done | bytes 163872 | tf_op jit(solution)/shard_map/ppermute | solution.py:45
  43.1 1.9 collective-permute-start.3
  45.0 6.5 %collective-permute-done.3 = bf16[128,640]{0,1:T(8,128)(2,1)S(1)} collective-permute-done((bf16[128,640]{0,1:T(8,128)(2,1)S(1)}, bf16[128,640]{0,1:T(8,128)(2,1)S(1)}, u32[]{:S(2)}, u32[]{:S(2)}) %collective-permute-start.3) | collective-permute-done | bytes 163872 | tf_op jit(solution)/shard_map/ppermute | solution.py:45
  52.1 1.9 collective-permute-start.4
  54.1 6.5 %collective-permute-done.4 = bf16[128,640]{0,1:T(8,128)(2,1)S(1)} collective-permute-done((bf16[128,640]{0,1:T(8,128)(2,1)S(1)}, bf16[128,640]{0,1:T(8,128)(2,1)S(1)}, u32[]{:S(2)}, u32[]{:S(2)}) %collective-permute-start.4) | collective-permute-done | bytes 163872 | tf_op jit(solution)/shard_map/ppermute | solution.py:45
  61.2 1.9 collective-permute-start.5
  63.1 6.6 %collective-permute-done.5 = bf16[128,640]{0,1:T(8,128)(2,1)S(1)} collective-permute-done((bf16[128,640]{0,1:T(8,128)(2,1)S(1)}, bf16[128,640]{0,1:T(8,128)(2,1)S(1)}, u32[]{:S(2)}, u32[]{:S(2)}) %collective-permute-start.5) | collective-permute-done | bytes 163872 | tf_op jit(solution)/shard_map/ppermute | solution.py:45
  70.4 1.9 collective-permute-start.6
  72.3 7.8 %collective-permute-done.6 = bf16[128,640]{0,1:T(8,128)(2,1)S(1)} collective-permute-done((bf16[128,640]{0,1:T(8,128)(2,1)S(1)}, bf16[128,640]{0,1:T(8,128)(2,1)S(1)}, u32[]{:S(2)}, u32[]{:S(2)}) %collective-permute-start.6) | collective-permute-done | bytes 163872 | tf_op jit(solution)/shard_map/ppermute | solution.py:45
  80.8 1.9 collective-permute-start.7
  82.7 7.5 %collective-permute-done.7 = bf16[128,640]{0,1:T(8,128)(2,1)S(1)} collective-permute-done((bf16[128,640]{0,1:T(8,128)(2,1)S(1)}, bf16[128,640]{0,1:T(8,128)(2,1)S(1)}, u32[]{:S(2)}, u32[]{:S(2)}) %collective-permute-start.7) | collective-permute-done | bytes 163872 | tf_op jit(solution)/shard_map/ppermute | solution.py:45
  90.9 1.9 collective-permute-start.8
  92.8 6.7 %collective-permute-done.8 = bf16[128,640]{0,1:T(8,128)(2,1)S(1)} collective-permute-done((bf16[128,640]{0,1:T(8,128)(2,1)S(1)}, bf16[128,640]{0,1:T(8,128)(2,1)S(1)}, u32[]{:S(2)}, u32[]{:S(2)}) %collective-permute-start.8) | collective-permute-done | bytes 163872 | tf_op jit(solution)/shard_map/ppermute | solution.py:45
  100.2 1.9 collective-permute-start.9
  102.1 6.6 %collective-permute-done.9 = bf16[128,640]{0,1:T(8,128)(2,1)} collective-permute-done((bf16[128,640]{0,1:T(8,128)(2,1)S(1)}, bf16[128,640]{0,1:T(8,128)(2,1)}, u32[]{:S(2)}, u32[]{:S(2)}) %collective-permute-start.9) | collective-permute-done | bytes 163872 | tf_op jit(solution)/shard_map/ppermute | solution.py:45
  108.7 1.9 collective-permute-start.10
  110.7 6.7 %collective-permute-done.10 = bf16[128,640]{0,1:T(8,128)(2,1)} collective-permute-done((bf16[128,640]{0,1:T(8,128)(2,1)}, bf16[128,640]{0,1:T(8,128)(2,1)}, u32[]{:S(2)}, u32[]{:S(2)}) %collective-permute-start.10) | collective-permute-done | bytes 163872 | tf_op jit(solution)/shard_map/ppermute | solution.py:45
  117.4 1.9 collective-permute-start.11
  119.3 6.7 %collective-permute-done.11 = bf16[128,640]{0,1:T(8,128)(2,1)S(1)} collective-permute-done((bf16[128,640]{0,1:T(8,128)(2,1)}, bf16[128,640]{0,1:T(8,128)(2,1)S(1)}, u32[]{:S(2)}, u32[]{:S(2)}) %collective-permute-start.11) | collective-permute-done | bytes 163872 | tf_op jit(solution)/shard_map/ppermute | solution.py:45
  126.7 1.9 collective-permute-start.12
  128.6 9.0 %collective-permute-done.12 = bf16[128,640]{0,1:T(8,128)(2,1)S(1)} collective-permute-done((bf16[128,640]{0,1:T(8,128)(2,1)S(1)}, bf16[128,640]{0,1:T(8,128)(2,1)S(1)}, u32[]{:S(2)}, u32[]{:S(2)}) %collective-permute-start.12) | collective-permute-done | bytes 163872 | tf_op jit(solution)/shard_map/ppermute | solution.py:45
  138.2 1.9 collective-permute-start.13
  140.8 7.9 %collective-permute-done.13 = bf16[128,640]{0,1:T(8,128)(2,1)} collective-permute-done((bf16[128,640]{0,1:T(8,128)(2,1)S(1)}, bf16[128,640]{0,1:T(8,128)(2,1)}, u32[]{:S(2)}, u32[]{:S(2)}) %collective-permute-start.13) | collective-permute-done | bytes 163872 | tf_op jit(solution)/shard_map/ppermute | solution.py:45
  148.7 1.9 collective-permute-start.14
  150.6 1.7 copy.23
  153.2 1.2 select_reduce_fusion
  154.5 5.7 %collective-permute-done.14 = bf16[128,640]{0,1:T(8,128)(2,1)} collective-permute-done((bf16[128,640]{0,1:T(8,128)(2,1)}, bf16[128,640]{0,1:T(8,128)(2,1)}, u32[]{:S(2)}, u32[]{:S(2)}) %collective-permute-start.14) | collective-permute-done | bytes 163872 | tf_op jit(solution)/shard_map/ppermute | solution.py:45
  161.1 1.0 constant_dynamic-update-slice_fusion.30
  162.1 1.0 constant_dynamic-update-slice_fusion.29
  164.1 1.0 constant_dynamic-update-slice_fusion.27
  165.0 1.0 constant_dynamic-update-slice_fusion.26
  167.0 1.0 constant_dynamic-update-slice_fusion.24
  168.0 1.0 constant_dynamic-update-slice_fusion.23
  168.9 1.0 constant_dynamic-update-slice_fusion.22
  170.9 1.0 constant_dynamic-update-slice_fusion.20
  171.9 1.0 constant_dynamic-update-slice_fusion.19
  172.8 1.0 constant_dynamic-update-slice_fusion.18
  173.8 1.0 constant_dynamic-update-slice_fusion.17
  174.9 1.0 constant_dynamic-update-slice_fusion.15
  177.0 1.0 constant_dynamic-update-slice_fusion.11
  177.9 1.0 constant_dynamic-update-slice_fusion.10
  179.8 1.1 bitcast_reduce_fusion
  180.9 2.3 copy-done.1
  184.1 3.0 all-gather.7.cloned.1.call-done
  187.1 3.5 %fusion.14 = bf16[2,128,640]{2,1,0:T(8,128)(2,1)S(1)} fusion(bf16[1,2560,640]{2,1,0:T(8,128)(2,1)} %all-gather.7.cloned.1.call-done, bf16[1,2,128,2560]{3,2,1,0:T(8,128)(2,1)} %all-gather.5.cloned.1.call-done, f32[2560]{0:T(1024)S(1)} %add.35), kind=kOutput, calls=%fused_computation.19 | convolution fusion | flops 840990720 | bytes 4925440 | tf_op jit(solution)/shard_map/btd,dk->btk/dot_general | solution.py:36
  192.1 5.2 %convolution_convert_fusion.1 = bf16[5,128,2048]{2,1,0:T(8,128)(2,1)} fusion(bf16[128,5,128]{0,2,1:T(8,128)(2,1)} %bitcast.68, f32[5,2048,128]{2,1,0:T(8,128)} %copy-done.1, f32[5,128]{1,0:T(8,128)S(1)} %log_add_fusion), kind=kOutput, calls=%fused_computation.11 | convolution fusion | flops 340787200 | bytes 8030720 | tf_op jit(solution)/shard_map/hij,ihe->jhe/dot_general | solution.py:59
  197.3 4.4 %copy.27 = bf16[2048,640]{1,0:T(8,128)(2,1)} copy(bf16[2048,640]{0,1:T(8,128)(2,1)} %bitcast.61) | data formatting | bytes 5242880 | tf_op jit(solution)/shard_map/convert_element_type | solution.py:61
  201.9 71.0 %reduce-scatter.5.cloned.1.call-done = bf16[128,640]{1,0:T(8,128)(2,1)} async-done(((bf16[2048,640]{1,0:T(8,128)(2,1)}), bf16[128,640]{1,0:T(8,128)(2,1)}) %reduce-scatter.5.cloned.1.call-update) | async-done | bytes 163856 | tf_op jit(solution)/shard_map/reduce_scatter | solution.py:60
  272.9 3.2 convolution_convert_fusion
  276.1 4.3 %copy.31 = bf16[2,128,2560]{1,0,2:T(2,128)(2,1)} copy(bf16[2,128,2560]{2,1,0:T(8,128)(2,1)} %convolution_convert_fusion) | data formatting | bytes 2621440
  280.4 2.6 copy.35
  283.0 27.4 %reduce-scatter.7.cloned.1.call-done = bf16[640,256]{1,0:T(8,128)(2,1)} async-done(((bf16[2560,256]{1,0:T(8,128)(2,1)}), bf16[640,256]{1,0:T(8,128)(2,1)}) %reduce-scatter.7.cloned.1.call-update) | async-done | bytes 327696
  310.4 1.8 reshape.33
  312.2 1.9 copy.32
  314.1 1.9 fusion.19
  316.0 2.8 collective-permute-start.15
  319.7 11.8 %collective-permute-done.15 = bf16[2,128,640]{2,1,0:T(8,128)(2,1)} collective-permute-done((bf16[2,128,640]{2,1,0:T(8,128)(2,1)}, bf16[2,128,640]{2,1,0:T(8,128)(2,1)}, u32[]{:S(2)}, u32[]{:S(2)}) %collective-permute-start.15) | collective-permute-done | bytes 327712 | tf_op jit(solution)/shard_map/ppermute | solution.py:13
  331.5 1.7 fusion.22
  (87 shorter events, 18.0 us)
Async XLA Ops:
  6.5 266.3 %copy-start = (bf16[1,2560,640]{2,1,0:T(8,128)(2,1)S(1)}, bf16[1,2560,640]{2,1,0:T(8,128)(2,1)}, u32[]{:S(2)}) copy-start(bf16[1,2560,640]{2,1,0:T(8,128)(2,1)} %param.13) | copy-start | bytes 9830404
  6.5 177.6 %all-gather.5.cloned.1.call-start = ((), (), s32[]{:S(2)}) async-start(), calls=%async_computation.3 | async-start | bytes 1638400 | tf_op jit(solution)/shard_map/all_gather | solution.py:33
  7.3 179.8 %all-gather.7.cloned.1.call-start = ((), (), s32[]{:S(2)}) async-start(), calls=%async_computation.4 | async-start | bytes 3481600 | tf_op jit(solution)/shard_map/all_gather | solution.py:35
  8.6 15.6 %collective-permute-start = (bf16[128,640]{0,1:T(8,128)(2,1)S(1)}, bf16[128,640]{0,1:T(8,128)(2,1)S(1)}, u32[]{:S(2)}, u32[]{:S(2)}) collective-permute-start(bf16[128,640]{0,1:T(8,128)(2,1)S(1)} %bitcast.65), channel_id=1, source_target_pairs={{0,1},{1,2},{2,3},{3,4},{4,5},{5,6},{6,7},{7,8},{8,9},{9,10},{10,1... | collective-permute-start | bytes 491528 | tf_op jit(solution)/shard_map/ppermute | solution.py:45
  24.2 0.7 copy-start.2
  24.8 8.5 %collective-permute-start.1 = (bf16[128,640]{0,1:T(8,128)(2,1)S(1)}, bf16[128,640]{0,1:T(8,128)(2,1)S(1)}, u32[]{:S(2)}, u32[]{:S(2)}) collective-permute-start(bf16[128,640]{0,1:T(8,128)(2,1)S(1)} %collective-permute-done), channel_id=1, source_target_pairs={{0,1},{1,2},{2,3},{3,4},{4,5},{5,6},{6,7},{7,8},{8,9},{9,10},{10,1... | collective-permute-start | bytes 491528 | tf_op jit(solution)/shard_map/ppermute | solution.py:45
  33.3 0.7 copy-start.4
  34.0 8.4 %collective-permute-start.2 = (bf16[128,640]{0,1:T(8,128)(2,1)S(1)}, bf16[128,640]{0,1:T(8,128)(2,1)S(1)}, u32[]{:S(2)}, u32[]{:S(2)}) collective-permute-start(bf16[128,640]{0,1:T(8,128)(2,1)S(1)} %collective-permute-done.1), channel_id=1, source_target_pairs={{0,1},{1,2},{2,3},{3,4},{4,5},{5,6},{6,7},{7,8},{8,9},{9,10},{10,1... | collective-permute-start | bytes 491528 | tf_op jit(solution)/shard_map/ppermute | solution.py:45
  42.4 0.7 copy-start.6
  43.1 8.4 %collective-permute-start.3 = (bf16[128,640]{0,1:T(8,128)(2,1)S(1)}, bf16[128,640]{0,1:T(8,128)(2,1)S(1)}, u32[]{:S(2)}, u32[]{:S(2)}) collective-permute-start(bf16[128,640]{0,1:T(8,128)(2,1)S(1)} %collective-permute-done.2), channel_id=1, source_target_pairs={{0,1},{1,2},{2,3},{3,4},{4,5},{5,6},{6,7},{7,8},{8,9},{9,10},{10,1... | collective-permute-start | bytes 491528 | tf_op jit(solution)/shard_map/ppermute | solution.py:45
  51.5 0.7 copy-start.8
  52.1 8.4 %collective-permute-start.4 = (bf16[128,640]{0,1:T(8,128)(2,1)S(1)}, bf16[128,640]{0,1:T(8,128)(2,1)S(1)}, u32[]{:S(2)}, u32[]{:S(2)}) collective-permute-start(bf16[128,640]{0,1:T(8,128)(2,1)S(1)} %collective-permute-done.3), channel_id=1, source_target_pairs={{0,1},{1,2},{2,3},{3,4},{4,5},{5,6},{6,7},{7,8},{8,9},{9,10},{10,1... | collective-permute-start | bytes 491528 | tf_op jit(solution)/shard_map/ppermute | solution.py:45
  60.6 0.7 copy-start.10
  61.2 8.5 %collective-permute-start.5 = (bf16[128,640]{0,1:T(8,128)(2,1)S(1)}, bf16[128,640]{0,1:T(8,128)(2,1)S(1)}, u32[]{:S(2)}, u32[]{:S(2)}) collective-permute-start(bf16[128,640]{0,1:T(8,128)(2,1)S(1)} %collective-permute-done.4), channel_id=1, source_target_pairs={{0,1},{1,2},{2,3},{3,4},{4,5},{5,6},{6,7},{7,8},{8,9},{9,10},{10,1... | collective-permute-start | bytes 491528 | tf_op jit(solution)/shard_map/ppermute | solution.py:45
  69.7 0.7 copy-start.12
  70.4 9.7 %collective-permute-start.6 = (bf16[128,640]{0,1:T(8,128)(2,1)S(1)}, bf16[128,640]{0,1:T(8,128)(2,1)S(1)}, u32[]{:S(2)}, u32[]{:S(2)}) collective-permute-start(bf16[128,640]{0,1:T(8,128)(2,1)S(1)} %collective-permute-done.5), channel_id=1, source_target_pairs={{0,1},{1,2},{2,3},{3,4},{4,5},{5,6},{6,7},{7,8},{8,9},{9,10},{10,1... | collective-permute-start | bytes 491528 | tf_op jit(solution)/shard_map/ppermute | solution.py:45
  80.1 0.7 copy-start.14
  80.8 9.4 %collective-permute-start.7 = (bf16[128,640]{0,1:T(8,128)(2,1)S(1)}, bf16[128,640]{0,1:T(8,128)(2,1)S(1)}, u32[]{:S(2)}, u32[]{:S(2)}) collective-permute-start(bf16[128,640]{0,1:T(8,128)(2,1)S(1)} %collective-permute-done.6), channel_id=1, source_target_pairs={{0,1},{1,2},{2,3},{3,4},{4,5},{5,6},{6,7},{7,8},{8,9},{9,10},{10,1... | collective-permute-start | bytes 491528 | tf_op jit(solution)/shard_map/ppermute | solution.py:45
  90.2 0.7 copy-start.16
  90.9 8.6 %collective-permute-start.8 = (bf16[128,640]{0,1:T(8,128)(2,1)S(1)}, bf16[128,640]{0,1:T(8,128)(2,1)S(1)}, u32[]{:S(2)}, u32[]{:S(2)}) collective-permute-start(bf16[128,640]{0,1:T(8,128)(2,1)S(1)} %collective-permute-done.7), channel_id=1, source_target_pairs={{0,1},{1,2},{2,3},{3,4},{4,5},{5,6},{6,7},{7,8},{8,9},{9,10},{10,1... | collective-permute-start | bytes 491528 | tf_op jit(solution)/shard_map/ppermute | solution.py:45
  99.5 0.7 copy-start.18
  100.2 8.5 %collective-permute-start.9 = (bf16[128,640]{0,1:T(8,128)(2,1)S(1)}, bf16[128,640]{0,1:T(8,128)(2,1)}, u32[]{:S(2)}, u32[]{:S(2)}) collective-permute-start(bf16[128,640]{0,1:T(8,128)(2,1)S(1)} %collective-permute-done.8), channel_id=1, source_target_pairs={{0,1},{1,2},{2,3},{3,4},{4,5},{5,6},{6,7},{7,8},{8,9},{9,10},{10,1... | collective-permute-start | bytes 491528 | tf_op jit(solution)/shard_map/ppermute | solution.py:45
  108.7 8.7 %collective-permute-start.10 = (bf16[128,640]{0,1:T(8,128)(2,1)}, bf16[128,640]{0,1:T(8,128)(2,1)}, u32[]{:S(2)}, u32[]{:S(2)}) collective-permute-start(bf16[128,640]{0,1:T(8,128)(2,1)} %collective-permute-done.9), channel_id=1, source_target_pairs={{0,1},{1,2},{2,3},{3,4},{4,5},{5,6},{6,7},{7,8},{8,9},{9,10},{10,1... | collective-permute-start | bytes 491528 | tf_op jit(solution)/shard_map/ppermute | solution.py:45
  110.6 162.2 %reduce-scatter.5.cloned.1.call-start = ((), (), s32[]{:S(2)}) async-start(), calls=%async_computation.2 | async-start | bytes 2785280 | tf_op jit(solution)/shard_map/reduce_scatter | solution.py:60
  117.4 8.6 %collective-permute-start.11 = (bf16[128,640]{0,1:T(8,128)(2,1)}, bf16[128,640]{0,1:T(8,128)(2,1)S(1)}, u32[]{:S(2)}, u32[]{:S(2)}) collective-permute-start(bf16[128,640]{0,1:T(8,128)(2,1)} %collective-permute-done.10), channel_id=1, source_target_pairs={{0,1},{1,2},{2,3},{3,4},{4,5},{5,6},{6,7},{7,8},{8,9},{9,10},{10,1... | collective-permute-start | bytes 491528 | tf_op jit(solution)/shard_map/ppermute | solution.py:45
  126.0 0.7 copy-start.20
  126.7 10.9 %collective-permute-start.12 = (bf16[128,640]{0,1:T(8,128)(2,1)S(1)}, bf16[128,640]{0,1:T(8,128)(2,1)S(1)}, u32[]{:S(2)}, u32[]{:S(2)}) collective-permute-start(bf16[128,640]{0,1:T(8,128)(2,1)S(1)} %collective-permute-done.11), channel_id=1, source_target_pairs={{0,1},{1,2},{2,3},{3,4},{4,5},{5,6},{6,7},{7,8},{8,9},{9,10},{10,1... | collective-permute-start | bytes 491528 | tf_op jit(solution)/shard_map/ppermute | solution.py:45
  137.6 0.7 copy-start.22
  138.2 10.4 %collective-permute-start.13 = (bf16[128,640]{0,1:T(8,128)(2,1)S(1)}, bf16[128,640]{0,1:T(8,128)(2,1)}, u32[]{:S(2)}, u32[]{:S(2)}) collective-permute-start(bf16[128,640]{0,1:T(8,128)(2,1)S(1)} %collective-permute-done.12), channel_id=1, source_target_pairs={{0,1},{1,2},{2,3},{3,4},{4,5},{5,6},{6,7},{7,8},{8,9},{9,10},{10,1... | collective-permute-start | bytes 491528 | tf_op jit(solution)/shard_map/ppermute | solution.py:45
  148.7 11.5 %collective-permute-start.14 = (bf16[128,640]{0,1:T(8,128)(2,1)}, bf16[128,640]{0,1:T(8,128)(2,1)}, u32[]{:S(2)}, u32[]{:S(2)}) collective-permute-start(bf16[128,640]{0,1:T(8,128)(2,1)} %collective-permute-done.13), channel_id=1, source_target_pairs={{0,1},{1,2},{2,3},{3,4},{4,5},{5,6},{6,7},{7,8},{8,9},{9,10},{10,1... | collective-permute-start | bytes 491528 | tf_op jit(solution)/shard_map/ppermute | solution.py:45
  153.1 23.7 %copy-start.23 = (bf16[128,640]{0,1:T(8,128)(2,1)S(1)}, bf16[128,640]{0,1:T(8,128)(2,1)}, u32[]{:S(2)}) copy-start(bf16[128,640]{0,1:T(8,128)(2,1)} %copy-done.22) | copy-start | bytes 491524
  153.1 23.8 %copy-start.21 = (bf16[128,640]{0,1:T(8,128)(2,1)S(1)}, bf16[128,640]{0,1:T(8,128)(2,1)}, u32[]{:S(2)}) copy-start(bf16[128,640]{0,1:T(8,128)(2,1)} %copy-done.20) | copy-start | bytes 491524
  153.1 25.8 %copy-start.19 = (bf16[128,640]{0,1:T(8,128)(2,1)S(1)}, bf16[128,640]{0,1:T(8,128)(2,1)}, u32[]{:S(2)}) copy-start(bf16[128,640]{0,1:T(8,128)(2,1)} %copy-done.18) | copy-start | bytes 491524
  153.1 25.9 %copy-start.17 = (bf16[128,640]{0,1:T(8,128)(2,1)S(1)}, bf16[128,640]{0,1:T(8,128)(2,1)}, u32[]{:S(2)}) copy-start(bf16[128,640]{0,1:T(8,128)(2,1)} %copy-done.16) | copy-start | bytes 491524
  153.1 25.9 %copy-start.15 = (bf16[128,640]{0,1:T(8,128)(2,1)S(1)}, bf16[128,640]{0,1:T(8,128)(2,1)}, u32[]{:S(2)}) copy-start(bf16[128,640]{0,1:T(8,128)(2,1)} %copy-done.14) | copy-start | bytes 491524
  153.2 26.0 %copy-start.13 = (bf16[128,640]{0,1:T(8,128)(2,1)S(1)}, bf16[128,640]{0,1:T(8,128)(2,1)}, u32[]{:S(2)}) copy-start(bf16[128,640]{0,1:T(8,128)(2,1)} %copy-done.12) | copy-start | bytes 491524
  153.2 26.0 %copy-start.11 = (bf16[128,640]{0,1:T(8,128)(2,1)S(1)}, bf16[128,640]{0,1:T(8,128)(2,1)}, u32[]{:S(2)}) copy-start(bf16[128,640]{0,1:T(8,128)(2,1)} %copy-done.10) | copy-start | bytes 491524
  153.2 26.1 %copy-start.9 = (bf16[128,640]{0,1:T(8,128)(2,1)S(1)}, bf16[128,640]{0,1:T(8,128)(2,1)}, u32[]{:S(2)}) copy-start(bf16[128,640]{0,1:T(8,128)(2,1)} %copy-done.8) | copy-start | bytes 491524
  153.2 26.1 %copy-start.7 = (bf16[128,640]{0,1:T(8,128)(2,1)S(1)}, bf16[128,640]{0,1:T(8,128)(2,1)}, u32[]{:S(2)}) copy-start(bf16[128,640]{0,1:T(8,128)(2,1)} %copy-done.6) | copy-start | bytes 491524
  153.2 26.2 %copy-start.5 = (bf16[128,640]{0,1:T(8,128)(2,1)S(1)}, bf16[128,640]{0,1:T(8,128)(2,1)}, u32[]{:S(2)}) copy-start(bf16[128,640]{0,1:T(8,128)(2,1)} %copy-done.4) | copy-start | bytes 491524
  153.2 26.3 %copy-start.3 = (bf16[128,640]{0,1:T(8,128)(2,1)S(1)}, bf16[128,640]{0,1:T(8,128)(2,1)}, u32[]{:S(2)}) copy-start(bf16[128,640]{0,1:T(8,128)(2,1)} %copy-done.2) | copy-start | bytes 491524
  174.8 5.0 %copy-start.24 = (bf16[1,128,640]{1,2,0:T(8,128)(2,1)S(1)}, bf16[1,128,640]{1,2,0:T(8,128)(2,1)}, u32[]{:S(2)}) copy-start(bf16[1,128,640]{1,2,0:T(8,128)(2,1)} %copy.23) | copy-start | bytes 491524
  180.9 2.3 copy-start.1
  197.3 75.5 %copy-start.25 = (bf16[1,128,640]{2,1,0:T(8,128)(2,1)S(1)}, bf16[1,128,640]{2,1,0:T(8,128)(2,1)}, u32[]{:S(2)}) copy-start(bf16[1,128,640]{2,1,0:T(8,128)(2,1)} %get-tuple-element.6) | copy-start | bytes 491524
  201.8 108.6 %reduce-scatter.7.cloned.1.call-start = ((), (), s32[]{:S(2)}) async-start(), calls=%async_computation.5 | async-start | bytes 1638400
  316.0 15.5 %collective-permute-start.15 = (bf16[2,128,640]{2,1,0:T(8,128)(2,1)}, bf16[2,128,640]{2,1,0:T(8,128)(2,1)}, u32[]{:S(2)}, u32[]{:S(2)}) collective-permute-start(bf16[2,128,640]{2,1,0:T(8,128)(2,1)} %fusion.19), channel_id=1, source_target_pairs={{64,0},{128,64},{192,128},{256,192},{320,256},{384,320},{448,384},... | collective-permute-start | bytes 983048 | tf_op jit(solution)/shard_map/ppermute | solution.py:13
Sparse Core Ops, SparseCore 0:
  9.5 34.6 all-gather.4
  110.7 76.3 all-gather.6
  201.9 70.8 reduce-scatter.4
  283.1 27.2 reduce-scatter.6
